TPU v7x, 256 devices: a whole 4x4x8 slice. The times are simulated.
256 devices in a mesh: grp: 4 (over y), tok: 64 (over z, x, core).
Axes of the slice: x: 4, y: 4, z: 8, core: 2. Of those that a mesh axis runs over, the one named last changes fastest.
Arguments:
- hidden: bfloat16 [512, 64, 1024], P('tok', 'grp'), may hold values from -6 to 6
- draft_qkv: bfloat16 [3, 512, 64, 1024], P(None, 'tok', None, 'grp'), may hold values from -4 to 4
- self_cache: bfloat16 [512, 2, 512, 1024], P('tok', None, None, 'grp'), may hold values from -4 to 4
- cross_cache: bfloat16 [512, 2, 512, 1024], P('tok', None, None, 'grp'), may hold values from -4 to 4
- parents: int32 [512, 64], P('tok'), may hold values from -1 to 62, as said below
- counts: int32 [512], P('tok'), may hold values from 32 to 64, as said below
- self_len: int32 [512], P('tok'), may hold values from 2 to 512, as said below
- enc_len: int32 [512], P('tok'), may hold values from 2 to 512, as said below
- buckets: int32 [512, 64, 64], P('tok'), may hold values from 0 to 31
- bias_table: float32 [32, 16], P(None, 'grp'), may hold values from -4 to 4
- gain_cross: float32 [1024], replicated, may hold values from 0.25 to 1.75
- gain_ffn: float32 [1024], replicated, may hold values from 0.25 to 1.75
- gain_next: float32 [1024], replicated, may hold values from 0.25 to 1.75
- w_out_self: bfloat16 [1024, 1024], P('grp', 'tok'), may hold values from -0.1875 to 0.1875
- w_query_cross: bfloat16 [1024, 1024], P('tok', 'grp'), may hold values from -1 to 1
- w_out_cross: bfloat16 [1024, 1024], P('grp', 'tok'), may hold values from -0.1875 to 0.1875
- w_gate: bfloat16 [1024, 2816], P('tok', 'grp'), may hold values from -0.1875 to 0.1875
- w_up: bfloat16 [1024, 2816], P('tok', 'grp'), may hold values from -0.1875 to 0.1875
- w_down: bfloat16 [2816, 1024], P('grp', 'tok'), may hold values from -0.109375 to 0.109375
- w_qkv: bfloat16 [1024, 3, 1024], P('tok', None, 'grp'), may hold values from -0.1875 to 0.1875
Outputs:
- out_hidden: bfloat16 [512, 64, 1024], P('tok', 'grp')
- next_qkv: bfloat16 [3, 512, 64, 1024], P(None, 'tok', None, 'grp')
Inputs may be any that keep to these rules, and one draw needn't show every extreme that they name: `parents`: slot 0 of every tree has parent -1; every other slot's parent is an earlier slot. `counts`: some request fills all 64 draft slots. `self_len`: some request fills its whole cache. `enc_len`: some request has all 512 encoder positions.
All inputs are finite; a program needn't handle non-finite values.
Results may differ from a plain program's by a relative error of at most 0.025.
Values may be sent and summed in bfloat16 or wider, within the bound.
A program may use at most 64 MiB of HBM per device.

v0:
```python
import jax
import jax.numpy as jnp
from jax import lax
from jax.sharding import PartitionSpec as P

DH = 64


def ancestor_table(parent_ids):
    count_slots = parent_ids.shape[0]
    slot_ids = jnp.arange(count_slots, dtype=jnp.int32)
    ancestors = jnp.eye(count_slots, dtype=jnp.float32) + (
        parent_ids[:, None] == slot_ids[None, :]
    ).astype(jnp.float32)
    for repeat in range(max(1, count_slots.bit_length())):
        ancestors = jnp.minimum(jnp.dot(ancestors, ancestors, precision=lax.Precision.HIGHEST), 1.0)
    return ancestors


def rms_scale(stream, gain_vec):
    mean_square = jnp.mean(stream * stream, axis=-1, keepdims=True)
    return (stream * lax.rsqrt(mean_square + 1e-06) * gain_vec).astype(jnp.bfloat16)


def draft_attention(projected, cached, parent_ids, draft_count, length, bucket_ids, bias_table):
    requests, draft_slots, head_width = (projected.shape[1], projected.shape[2], projected.shape[3])
    local_heads = bias_table.shape[1]
    head_size = head_width // local_heads
    queries = projected[0].reshape(requests, draft_slots, local_heads, head_size)
    draft_keys = projected[1].reshape(requests, draft_slots, local_heads, head_size)
    draft_values = projected[2].reshape(requests, draft_slots, local_heads, head_size)
    cache_keys = cached[:, 0].reshape(requests, -1, local_heads, head_size)
    cache_values = cached[:, 1].reshape(requests, -1, local_heads, head_size)
    cache_scores = jnp.einsum(
        "rihd,rphd->rhip", queries, cache_keys, preferred_element_type=jnp.float32
    )
    cache_scores = cache_scores + bias_table[-1][None, :, None, None]
    cache_live = jnp.arange(cache_keys.shape[1], dtype=jnp.int32)[None, :] < length[:, None]
    cache_scores = jnp.where(cache_live[:, None, None, :], cache_scores, -1e30)
    onehot = (bucket_ids[..., None] == jnp.arange(bias_table.shape[0], dtype=jnp.int32)).astype(
        jnp.float32
    )
    draft_bias = jnp.einsum("rijb,bh->rhij", onehot, bias_table, precision=lax.Precision.HIGHEST)
    draft_scores = (
        jnp.einsum("rihd,rjhd->rhij", queries, draft_keys, preferred_element_type=jnp.float32)
        + draft_bias
    )
    ancestors = jax.vmap(ancestor_table)(parent_ids)
    draft_live = (ancestors > 0.5) & (
        jnp.arange(draft_slots, dtype=jnp.int32)[None, None, :] < draft_count[:, None, None]
    )
    draft_scores = jnp.where(draft_live[:, None], draft_scores, -1e30)
    highest = jnp.maximum(cache_scores.max(-1, keepdims=True), draft_scores.max(-1, keepdims=True))
    exp_cache = jnp.exp(cache_scores - highest)
    exp_draft = jnp.exp(draft_scores - highest)
    denominator = exp_cache.sum(-1, keepdims=True) + exp_draft.sum(-1, keepdims=True)
    weights_cache = (exp_cache / denominator).astype(jnp.bfloat16)
    weights_draft = (exp_draft / denominator).astype(jnp.bfloat16)
    attended = jnp.einsum(
        "rhip,rphd->rihd", weights_cache, cache_values, preferred_element_type=jnp.float32
    )
    attended = attended + jnp.einsum(
        "rhij,rjhd->rihd", weights_draft, draft_values, preferred_element_type=jnp.float32
    )
    return attended.astype(jnp.bfloat16).reshape(requests * draft_slots, head_width)


def cross_attention(query_rows, cached, length):
    requests, draft_slots, head_width = query_rows.shape
    local_heads = head_width // DH
    queries = query_rows.reshape(requests, draft_slots, local_heads, DH)
    enc_keys = cached[:, 0].reshape(requests, -1, local_heads, DH)
    enc_values = cached[:, 1].reshape(requests, -1, local_heads, DH)
    scores = jnp.einsum("rihd,rphd->rhip", queries, enc_keys, preferred_element_type=jnp.float32)
    live = jnp.arange(enc_keys.shape[1], dtype=jnp.int32)[None, :] < length[:, None]
    scores = jnp.where(live[:, None, None, :], scores, -1e30)
    highest = scores.max(-1, keepdims=True)
    exp_scores = jnp.exp(scores - highest)
    weights = (exp_scores / exp_scores.sum(-1, keepdims=True)).astype(jnp.bfloat16)
    attended = jnp.einsum(
        "rhip,rphd->rihd", weights, enc_values, preferred_element_type=jnp.float32
    )
    return attended.astype(jnp.bfloat16).reshape(requests * draft_slots, head_width)


def layer_sum(summand, base_full):
    return lax.psum(summand.astype(jnp.bfloat16), "grp").astype(jnp.float32) + base_full


def normed_rows(stream, gain_vec):
    scaled = rms_scale(stream, gain_vec)
    return scaled.reshape(-1, scaled.shape[-1])


def shards(
    hidden,
    draft_qkv,
    self_cache,
    cross_cache,
    parents,
    counts,
    self_len,
    enc_len,
    buckets,
    bias_table,
    gain_cross,
    gain_ffn,
    gain_next,
    w_out_self,
    w_query_cross,
    w_out_cross,
    w_gate,
    w_up,
    w_down,
    w_qkv,
):
    requests, share_rows, model_width = hidden.shape
    draft_slots = draft_qkv.shape[2]
    head_width = draft_qkv.shape[3]
    fetched = (
        lax.all_gather(w_out_self, "tok", axis=1, tiled=True),
        lax.all_gather(w_query_cross, "tok", axis=0, tiled=True),
        lax.all_gather(w_out_cross, "tok", axis=1, tiled=True),
        lax.all_gather(w_gate, "tok", axis=0, tiled=True),
        lax.all_gather(w_up, "tok", axis=0, tiled=True),
        lax.all_gather(w_down, "tok", axis=1, tiled=True),
        lax.all_gather(w_qkv, "tok", axis=0, tiled=True),
    )
    self_context = draft_attention(
        draft_qkv, self_cache, parents, counts, self_len, buckets, bias_table
    )
    partial_value = jnp.dot(self_context, fetched[0], preferred_element_type=jnp.float32)
    partial_value = partial_value.reshape(requests, draft_slots, model_width)
    own_rows = hidden.astype(jnp.float32)
    offset = lax.axis_index("grp") * share_rows
    placed = lax.dynamic_update_slice(
        jnp.zeros((requests, draft_slots, model_width), jnp.float32), own_rows, (0, offset, 0)
    )
    stream_one = layer_sum(partial_value + placed, 0.0)
    normed_one = normed_rows(stream_one, gain_cross)
    cross_query = jnp.dot(normed_one, fetched[1], preferred_element_type=jnp.float32)
    cross_query = cross_query.astype(jnp.bfloat16).reshape(requests, draft_slots, head_width)
    cross_context = cross_attention(cross_query, cross_cache, enc_len)
    partial_value = jnp.dot(cross_context, fetched[2], preferred_element_type=jnp.float32)
    stream_two = layer_sum(partial_value.reshape(requests, draft_slots, model_width), stream_one)
    normed_two = normed_rows(stream_two, gain_ffn)
    gate_part = jnp.dot(normed_two, fetched[3], preferred_element_type=jnp.float32)
    up_part = jnp.dot(normed_two, fetched[4], preferred_element_type=jnp.float32)
    gated = (jax.nn.gelu(gate_part, approximate=True) * up_part).astype(jnp.bfloat16)
    partial_value = jnp.dot(gated, fetched[5], preferred_element_type=jnp.float32)
    stream_three = layer_sum(partial_value.reshape(requests, draft_slots, model_width), stream_two)
    normed_three = normed_rows(stream_three, gain_next)
    projected = jnp.dot(
        normed_three,
        fetched[6].reshape(fetched[6].shape[0], -1),
        preferred_element_type=jnp.float32,
    )
    projected = projected.astype(jnp.bfloat16).reshape(requests, draft_slots, 3, head_width)
    next_qkv = jnp.transpose(projected, (2, 0, 1, 3))
    out_hidden = lax.dynamic_slice_in_dim(stream_three, offset, share_rows, 1).astype(jnp.bfloat16)
    return (out_hidden, next_qkv)


def solution(mesh):
    in_specs = (
        P("tok", "grp", None),
        P(None, "tok", None, "grp"),
        P("tok", None, None, "grp"),
        P("tok", None, None, "grp"),
        P("tok", None),
        P("tok"),
        P("tok"),
        P("tok"),
        P("tok", None, None),
        P(None, "grp"),
        P(),
        P(),
        P(),
        P("grp", "tok"),
        P("tok", "grp"),
        P("grp", "tok"),
        P("tok", "grp"),
        P("tok", "grp"),
        P("grp", "tok"),
        P("tok", None, "grp"),
    )
    out_specs = (P("tok", "grp", None), P(None, "tok", None, "grp"))
    return jax.shard_map(shards, mesh=mesh, in_specs=in_specs, out_specs=out_specs, check_vma=False)
```

profile of v0, /device:TPU:1, one launch (start us, length us, event | category | flops | bytes accessed | tf_op | source)
XLA Modules:
  0.0 532.7 jit_solution(6397232074818495033)
XLA Ops:
  8.1 3.9 fusion.56
  12.0 2.4 copy.53
  14.6 2.9 copy.47
  17.5 1.9 fusion.57
  19.7 3.6 fusion.1
  23.3 2.6 copy.52
  25.8 1.2 reshape_squeeze.23
  32.0 1.5 fusion.7
  33.7 1.0 reshape_squeeze.25
  34.7 3.0 fusion.14
  39.0 54.8 %all_gather.21 = bf16[256,1024]{0,1:T(8,128)(2,1)S(1)} all-gather(bf16[256,16]{0,1:T(8,128)(2,1)S(1)} %copy-done.9), channel_id=1, replica_groups=mesh['grp'=4,'tok'=64] {'tok'}, dimensions={1}, use_global_device_ids=true | all-gather | bytes 532480 | tf_op jit(solution)/shard_map/all_gather | solution.py:121
  94.4 1.1 convert_element_type.84
  95.6 3.9 fusion.55
  99.5 2.4 copy.59
  101.9 2.9 copy.57
  104.8 49.2 %all_gather.22 = bf16[1024,256]{1,0:T(8,128)(2,1)S(1)} all-gather(bf16[16,256]{1,0:T(8,128)(2,1)S(1)} %copy-done.10), channel_id=1, replica_groups=mesh['grp'=4,'tok'=64] {'tok'}, dimensions={0}, use_global_device_ids=true | all-gather | bytes 532480 | tf_op jit(solution)/shard_map/all_gather | solution.py:122
  154.0 48.2 %all_gather.23 = bf16[256,1024]{0,1:T(8,128)(2,1)S(1)} all-gather(bf16[256,16]{0,1:T(8,128)(2,1)S(1)} %copy-done.11), channel_id=1, replica_groups=mesh['grp'=4,'tok'=64] {'tok'}, dimensions={1}, use_global_device_ids=true | all-gather | bytes 532480 | tf_op jit(solution)/shard_map/all_gather | solution.py:123
  202.2 1.5 fusion.8
  203.8 1.5 fusion.10
  206.7 2.0 fusion.59
  210.2 1.5 convolution_convert_fusion.1
  214.6 44.3 %all-reduce.6.cloned.1.call-done = bf16[8,64,1024]{2,1,0:T(8,128)(2,1)} async-done(((bf16[8,64,1024]{2,1,0:T(8,128)(2,1)}), bf16[8,64,1024]{2,1,0:T(8,128)(2,1)}) %all-reduce.6.cloned.1.call-update) | async-done | bytes 1048592 | tf_op jit(solution)/shard_map/psum | solution.py:87
  258.9 1.7 multiply_reduce_fusion.1
  261.0 28.7 %all-gather.5.cloned.1.call-done = bf16[1024,704]{1,0:T(8,128)(2,1)} async-done(((bf16[16,704]{1,0:T(8,128)(2,1)}), bf16[1024,704]{1,0:T(8,128)(2,1)}) %all-gather.5.cloned.1.call-update) | async-done | bytes 1441808 | tf_op jit(solution)/shard_map/all_gather | solution.py:124
  289.7 3.5 fusion.60
  293.2 73.9 %all-gather.9.cloned.1.call-done = bf16[704,1024]{0,1:T(8,128)(2,1)} async-done(((bf16[704,16]{0,1:T(8,128)(2,1)}), bf16[704,1024]{0,1:T(8,128)(2,1)}) %all-gather.9.cloned.1.call-update) | async-done | bytes 1441808 | tf_op jit(solution)/shard_map/all_gather | solution.py:126
  367.1 77.4 %all-gather.7.cloned.1.call-done = bf16[1024,704]{1,0:T(8,128)(2,1)} async-done(((bf16[16,704]{1,0:T(8,128)(2,1)}), bf16[1024,704]{1,0:T(8,128)(2,1)}) %all-gather.7.cloned.1.call-update) | async-done | bytes 1441808 | tf_op jit(solution)/shard_map/all_gather | solution.py:125
  444.5 5.5 %convolution_convert_fusion = bf16[512,1024]{1,0:T(8,128)(2,1)} fusion(bf16[704,1024]{0,1:T(8,128)(2,1)} %all-gather.9.cloned.1.call-done, bf16[512,1024]{1,0:T(8,128)(2,1)S(1)} %bitcast.67, bf16[1024,704]{1,0:T(8,128)(2,1)} %all-gather.7.cloned.1.call-done, f32[512,704]{0,1:T(8,128)} %fusion.60), kind=kOutput, calls=%fused_computation.29 | convolution fusion | flops 1480523776 | bytes 6422528 | tf_op jit(solution)/shard_map/dot_general | solution.py:150
  450.0 67.0 %all-gather.11.cloned.1.call-done = bf16[1024,3,256]{2,0,1:T(8,128)(2,1)} async-done(((bf16[16,3,256]{2,0,1:T(8,128)(2,1)}), bf16[1024,3,256]{2,0,1:T(8,128)(2,1)}) %all-gather.11.cloned.1.call-update) | async-done | bytes 1572880 | tf_op jit(solution)/shard_map/all_gather | solution.py:127
  517.1 2.6 copy.61
  519.7 1.8 multiply_reduce_fusion
  522.9 1.0 convolution_convert_fusion.2
  (96 shorter events, 16.4 us)
Async XLA Ops:
  8.0 194.2 %all-reduce.4.cloned.1.call-start = ((), (), s32[]{:S(2)}) async-start(), calls=%async_computation | async-start | bytes 2097152 | tf_op jit(solution)/shard_map/psum | solution.py:87
  12.0 2.4 copy-start.16
  12.0 2.6 copy-start.17
  17.5 2.2 copy-start.19
  19.7 7.4 %copy-start.12 = (s32[8,64]{1,0:T(8,128)S(1)}, s32[8,64]{1,0:T(8,128)}, u32[]{:S(2)}) copy-start(s32[8,64]{1,0:T(8,128)} %param.24) | copy-start | bytes 6148
  27.1 2.5 copy-start.20
  30.3 1.2 copy-start.3
  31.5 2.0 copy-start.1
  31.9 2.8 copy-start.4
  34.7 3.1 copy-start.7
  37.8 1.2 copy-start.9
  38.6 55.7 %copy-start.8 = (bf16[8,16,1024]{2,1,0:T(8,128)(2,1)S(1)}, bf16[8,16,1024]{2,1,0:T(8,128)(2,1)}, u32[]{:S(2)}) copy-start(bf16[8,16,1024]{2,1,0:T(8,128)(2,1)} %param.20) | copy-start | bytes 786436
  95.6 163.3 %all-reduce.6.cloned.1.call-start = ((), (), s32[]{:S(2)}) async-start(), calls=%async_computation.1 | async-start | bytes 2097152 | tf_op jit(solution)/shard_map/psum | solution.py:87
  101.9 2.9 copy-start.10
  101.9 52.1 %copy-start.11 = (bf16[256,16]{0,1:T(8,128)(2,1)S(1)}, bf16[256,16]{0,1:T(8,128)(2,1)}, u32[]{:S(2)}) copy-start(bf16[256,16]{0,1:T(8,128)(2,1)} %param.35) | copy-start | bytes 24580
  101.9 100.3 %copy-start.18 = (s32[8]{0:T(128)S(1)}, s32[8]{0:T(128)}, u32[]{:S(2)}) copy-start(s32[8]{0:T(128)} %param.27) | copy-start | bytes 100
  104.8 98.9 %copy-start.13 = (f32[1024]{0:T(1024)S(1)}, f32[1024]{0:T(1024)}, u32[]{:S(2)}) copy-start(f32[1024]{0:T(1024)} %param.30) | copy-start | bytes 12292
  206.7 2.0 copy-start.5
  209.9 49.0 %copy-start = (bf16[8,64,1024]{2,1,0:T(8,128)(2,1)S(1)}, bf16[8,64,1024]{2,1,0:T(8,128)(2,1)}, u32[]{:S(2)}) copy-start(bf16[8,64,1024]{2,1,0:T(8,128)(2,1)} %all-reduce.4.cloned.1.call-done) | copy-start | bytes 3145732
  210.2 50.4 %copy-start.14 = (f32[1024]{0:T(1024)S(1)}, f32[1024]{0:T(1024)}, u32[]{:S(2)}) copy-start(f32[1024]{0:T(1024)} %param.31) | copy-start | bytes 12292
  211.8 77.9 %all-gather.5.cloned.1.call-start = ((), (), s32[]{:S(2)}) async-start(), calls=%async_computation.2 | async-start | bytes 1597440 | tf_op jit(solution)/shard_map/all_gather | solution.py:124
  212.4 154.7 %all-gather.9.cloned.1.call-start = ((), (), s32[]{:S(2)}) async-start(), calls=%async_computation.4 | async-start | bytes 1597440 | tf_op jit(solution)/shard_map/all_gather | solution.py:126
  213.0 231.5 %all-gather.7.cloned.1.call-start = ((), (), s32[]{:S(2)}) async-start(), calls=%async_computation.3 | async-start | bytes 1597440 | tf_op jit(solution)/shard_map/all_gather | solution.py:125
  213.5 303.5 %all-gather.11.cloned.1.call-start = ((), (), s32[]{:S(2)}) async-start(), calls=%async_computation.6 | async-start | bytes 1597440 | tf_op jit(solution)/shard_map/all_gather | solution.py:127
  214.3 305.4 %all-reduce.8.cloned.1.call-start = ((), (), s32[]{:S(2)}) async-start(), calls=%async_computation.5 | async-start | bytes 2097152 | tf_op jit(solution)/shard_map/psum | solution.py:87
  258.9 1.7 copy-start.2
  519.6 2.5 copy-start.15
  521.4 1.5 copy-start.6
Sparse Core Ops, SparseCore 0:
  95.7 46.8 all-reduce.3
  211.9 46.8 all-reduce.5
  450.1 46.8 all-reduce.7
Sparse Core Ops, SparseCore 1:
  215.0 74.7 all-gather.4
  292.4 74.7 all-gather.8
  369.8 74.7 all-gather.6
  447.5 69.5 all-gather.10
where the time goes:
time: 533 us
  waiting for transfers between devices  294 us (55%)
  blocking collectives  152 us (29%)
  local copies, waits for them, and re-layouts  33.2 us (6%)
  matrix products  25 us (5%)
  between operations  15.9 us (3%)
  other arithmetic  12.3 us (2%)
    all_gather x1, waiting for transfers between devices, shards(): lax.all_gather(w_up, 'tok', axis=0, tiled=True)  77.4 us
    all_gather x1, waiting for transfers between devices, shards(): lax.all_gather(w_down, 'tok', axis=1, tiled=True)  73.9 us
    all_gather x1, waiting for transfers between devices, shards(): lax.all_gather(w_qkv, 'tok', axis=0, tiled=True)  67 us
    all_gather x1, blocking collectives, shards(): lax.all_gather(w_out_self, 'tok', axis=1, tiled=True)  54.8 us
    all_gather x1, blocking collectives, shards(): lax.all_gather(w_query_cross, 'tok', axis=0, tiled=True)  49.2 us
    all_gather x1, blocking collectives, shards(): lax.all_gather(w_out_cross, 'tok', axis=1, tiled=True)  48.2 us
    psum x3, waiting for transfers between devices, layer_sum(): lax.psum(summand.astype(jnp.bfloat16), 'grp').astype(jnp.float32)  44.3 us
    all_gather x1, waiting for transfers between devices, shards(): lax.all_gather(w_gate, 'tok', axis=0, tiled=True)  28.7 us
  transfers between devices with their start and end apart: 7, of which 5 were waited for; matrix products, arithmetic and copies ran while one was open for 4% of the time, Pallas kernels for 0%

commit v1 on v0

--- a/solution.py
+++ b/solution.py
@@ -84,7 +84,10 @@
 
 
 def layer_sum(summand, base_full):
-    return lax.psum(summand.astype(jnp.bfloat16), "grp").astype(jnp.float32) + base_full
+    return (
+        jnp.sum(lax.all_gather(summand.astype(jnp.bfloat16), "grp"), axis=0).astype(jnp.float32)
+        + base_full
+    )
 
 
 def normed_rows(stream, gain_vec):

time: 533 us -> 645 us (1.21)
  waiting for transfers between devices: 294 us -> 390 us
  blocking collectives: 152 us -> 161 us
    all_gather x0 -> x3, waiting for transfers between devices: none -> 94.3 us  [layer_sum(): lax.all_gather(summand.astype(jnp.bfloat16), 'grp')]
    all_gather x1, waiting for transfers between devices: 28.7 us -> 76.1 us  [shards(): lax.all_gather(w_gate, 'tok', axis=0, tiled=True)]
    psum x3 -> x0, waiting for transfers between devices: 44.3 us -> none  [layer_sum(): lax.psum(summand.astype(jnp.bfloat16), 'grp').astype(jnp.float32)]
    reduce_sum x0 -> x3, other arithmetic: none -> 9.84 us  [layer_sum(): jnp.sum(lax.all_gather(summand.astype(jnp.bfloat16), 'grp'), axis=0)]
  transfers between devices with their start and end apart: 7 -> 7, of which waited for: 5 -> 6; matrix products, arithmetic and copies ran while one was open for 4% -> 4% of each run, Pallas kernels for 0% -> 0%
where the time goes in v1:
time: 645 us
  waiting for transfers between devices  390 us (60%)
  blocking collectives  161 us (25%)
  local copies, waits for them, and re-layouts  35.4 us (5%)
  matrix products  25.9 us (4%)
  other arithmetic  17.3 us (3%)
  between operations  14.6 us (2%)
    all_gather x3, waiting for transfers between devices, layer_sum(): lax.all_gather(summand.astype(jnp.bfloat16), 'grp')  94.3 us
    all_gather x1, waiting for transfers between devices, shards(): lax.all_gather(w_up, 'tok', axis=0, tiled=True)  77.2 us
    all_gather x1, waiting for transfers between devices, shards(): lax.all_gather(w_gate, 'tok', axis=0, tiled=True)  76.1 us
    all_gather x1, waiting for transfers between devices, shards(): lax.all_gather(w_down, 'tok', axis=1, tiled=True)  73.7 us
    all_gather x1, waiting for transfers between devices, shards(): lax.all_gather(w_qkv, 'tok', axis=0, tiled=True)  66.2 us
    all_gather x1, blocking collectives, shards(): lax.all_gather(w_out_self, 'tok', axis=1, tiled=True)  54.8 us
    all_gather x1, blocking collectives, shards(): lax.all_gather(w_query_cross, 'tok', axis=0, tiled=True)  53.4 us
    all_gather x1, blocking collectives, shards(): lax.all_gather(w_out_cross, 'tok', axis=1, tiled=True)  52.9 us
  transfers between devices with their start and end apart: 7, of which 6 were waited for; matrix products, arithmetic and copies ran while one was open for 4% of the time, Pallas kernels for 0%

profile of v1, /device:TPU:1, one launch (start us, length us, event | category | flops | bytes accessed | tf_op | source)
XLA Modules:
  0.0 644.5 jit_solution(6770149965324391682)
XLA Ops:
  7.2 3.9 fusion.59
  11.1 2.4 copy.53
  13.8 2.9 copy.47
  16.7 1.9 fusion.60
  18.8 3.6 fusion.1
  22.4 2.6 copy.52
  25.0 1.2 reshape_squeeze.23
  31.1 1.5 fusion.7
  33.9 3.0 fusion.17
  38.2 54.8 %all_gather.37 = bf16[256,1024]{0,1:T(8,128)(2,1)S(1)} all-gather(bf16[256,16]{0,1:T(8,128)(2,1)S(1)} %copy-done.9), channel_id=1, replica_groups=mesh['grp'=4,'tok'=64] {'tok'}, dimensions={1}, use_global_device_ids=true | all-gather | bytes 532480 | tf_op jit(solution)/shard_map/all_gather | solution.py:124
  93.6 1.2 convert_element_type.146
  94.9 3.9 fusion.58
  98.8 2.4 copy.59
  101.2 2.9 copy.57
  104.1 53.4 %all_gather.40 = bf16[1024,256]{1,0:T(8,128)(2,1)} all-gather(bf16[16,256]{1,0:T(8,128)(2,1)S(1)} %copy-done.10), channel_id=1, replica_groups=mesh['grp'=4,'tok'=64] {'tok'}, dimensions={0}, use_global_device_ids=true | all-gather | bytes 532480 | tf_op jit(solution)/shard_map/all_gather | solution.py:125
  157.5 52.9 %all_gather.41 = bf16[256,1024]{0,1:T(8,128)(2,1)} all-gather(bf16[256,16]{0,1:T(8,128)(2,1)S(1)} %copy-done.11), channel_id=1, replica_groups=mesh['grp'=4,'tok'=64] {'tok'}, dimensions={1}, use_global_device_ids=true | all-gather | bytes 532480 | tf_op jit(solution)/shard_map/all_gather | solution.py:126
  210.5 3.3 reduce_sum.92
  215.7 1.0 reshape_reshape.3
  216.7 1.7 fusion.37
  218.5 2.0 fusion.62
  222.3 1.5 convolution_convert_fusion.1
  226.5 45.4 %all-gather.22.cloned.1.call-done = bf16[32,64,1024]{2,1,0:T(8,128)(2,1)} async-done(((bf16[8,64,1024]{2,1,0:T(8,128)(2,1)}), bf16[32,64,1024]{2,1,0:T(8,128)(2,1)}) %all-gather.22.cloned.1.call-update) | async-done | bytes 4194320 | tf_op jit(solution)/shard_map/all_gather | solution.py:88
  272.0 3.3 reduce_sum.95
  276.3 76.1 %all-gather.10.cloned.1.call-done = bf16[1024,704]{1,0:T(8,128)(2,1)} async-done(((bf16[16,704]{1,0:T(8,128)(2,1)}), bf16[1024,704]{1,0:T(8,128)(2,1)}) %all-gather.10.cloned.1.call-update) | async-done | bytes 1441808 | tf_op jit(solution)/shard_map/all_gather | solution.py:127
  352.4 3.5 fusion.63
  355.9 73.7 %all-gather.14.cloned.1.call-done = bf16[704,1024]{0,1:T(8,128)(2,1)} async-done(((bf16[704,16]{0,1:T(8,128)(2,1)}), bf16[704,1024]{0,1:T(8,128)(2,1)}) %all-gather.14.cloned.1.call-update) | async-done | bytes 1441808 | tf_op jit(solution)/shard_map/all_gather | solution.py:129
  429.6 77.2 %all-gather.12.cloned.1.call-done = bf16[1024,704]{1,0:T(8,128)(2,1)} async-done(((bf16[16,704]{1,0:T(8,128)(2,1)}), bf16[1024,704]{1,0:T(8,128)(2,1)}) %all-gather.12.cloned.1.call-update) | async-done | bytes 1441808 | tf_op jit(solution)/shard_map/all_gather | solution.py:128
  506.8 5.5 convolution_convert_fusion
  512.3 66.2 %all-gather.18.cloned.1.call-done = bf16[1024,3,256]{2,0,1:T(8,128)(2,1)} async-done(((bf16[16,3,256]{2,0,1:T(8,128)(2,1)}), bf16[1024,3,256]{2,0,1:T(8,128)(2,1)}) %all-gather.18.cloned.1.call-update) | async-done | bytes 1572880 | tf_op jit(solution)/shard_map/all_gather | solution.py:130
  578.5 2.6 copy.61
  581.1 48.8 %all-gather.16.cloned.1.call-done = bf16[4,8,64,1024]{3,2,1,0:T(8,128)(2,1)} async-done(((bf16[1,8,64,1024]{3,2,1,0:T(8,128)(2,1)}), bf16[4,8,64,1024]{3,2,1,0:T(8,128)(2,1)}) %all-gather.16.cloned.1.call-update) | async-done | bytes 4194320 | tf_op jit(solution)/shard_map/all_gather | solution.py:88
  629.9 3.3 reduce_sum.97
  (101 shorter events, 20.4 us)
Async XLA Ops:
  7.2 203.4 %all-gather.20.cloned.1.call-start = ((), (), s32[]{:S(2)}) async-start(), calls=%async_computation.5 | async-start | bytes 5242880 | tf_op jit(solution)/shard_map/all_gather | solution.py:88
  11.1 2.4 copy-start.16
  11.1 2.6 copy-start.17
  16.6 2.2 copy-start.19
  18.8 7.4 %copy-start.12 = (s32[8,64]{1,0:T(8,128)S(1)}, s32[8,64]{1,0:T(8,128)}, u32[]{:S(2)}) copy-start(s32[8,64]{1,0:T(8,128)} %param.24) | copy-start | bytes 6148
  26.3 2.5 copy-start.20
  29.4 1.2 copy-start.1
  30.6 2.0 copy-start
  31.1 2.8 copy-start.3
  33.9 3.1 copy-start.6
  36.9 1.2 copy-start.9
  37.8 55.7 %copy-start.8 = (bf16[8,16,1024]{2,1,0:T(8,128)(2,1)S(1)}, bf16[8,16,1024]{2,1,0:T(8,128)(2,1)}, u32[]{:S(2)}) copy-start(bf16[8,16,1024]{2,1,0:T(8,128)(2,1)} %param.20) | copy-start | bytes 786436
  94.8 177.1 %all-gather.22.cloned.1.call-start = ((), (), s32[]{:S(2)}) async-start(), calls=%async_computation.6 | async-start | bytes 5242880 | tf_op jit(solution)/shard_map/all_gather | solution.py:88
  101.2 3.0 copy-start.10
  101.2 56.3 %copy-start.11 = (bf16[256,16]{0,1:T(8,128)(2,1)S(1)}, bf16[256,16]{0,1:T(8,128)(2,1)}, u32[]{:S(2)}) copy-start(bf16[256,16]{0,1:T(8,128)(2,1)} %param.35) | copy-start | bytes 24580
  101.2 109.3 %copy-start.18 = (s32[8]{0:T(128)S(1)}, s32[8]{0:T(128)}, u32[]{:S(2)}) copy-start(s32[8]{0:T(128)} %param.27) | copy-start | bytes 100
  210.5 3.7 copy-start.13
  214.2 1.0 copy-start.7
  218.5 2.0 copy-start.4
  221.2 1.0 copy-start.2
  223.7 128.7 %all-gather.10.cloned.1.call-start = ((), (), s32[]{:S(2)}) async-start(), calls=%async_computation | async-start | bytes 1597440 | tf_op jit(solution)/shard_map/all_gather | solution.py:127
  224.5 205.2 %all-gather.14.cloned.1.call-start = ((), (), s32[]{:S(2)}) async-start(), calls=%async_computation.2 | async-start | bytes 1597440 | tf_op jit(solution)/shard_map/all_gather | solution.py:129
  225.1 281.8 %all-gather.12.cloned.1.call-start = ((), (), s32[]{:S(2)}) async-start(), calls=%async_computation.1 | async-start | bytes 1597440 | tf_op jit(solution)/shard_map/all_gather | solution.py:128
  225.6 352.9 %all-gather.18.cloned.1.call-start = ((), (), s32[]{:S(2)}) async-start(), calls=%async_computation.4 | async-start | bytes 1597440 | tf_op jit(solution)/shard_map/all_gather | solution.py:130
  226.2 403.7 %all-gather.16.cloned.1.call-start = ((), (), s32[]{:S(2)}) async-start(), calls=%async_computation.3 | async-start | bytes 5242880 | tf_op jit(solution)/shard_map/all_gather | solution.py:88
  275.3 0.7 copy-start.14
  633.2 1.3 copy-start.15
  633.7 1.5 copy-start.5
Sparse Core Ops, SparseCore 0:
  95.0 48.1 all-gather.19
  223.9 48.0 all-gather.21
  274.7 77.6 all-gather.9
  355.1 74.5 all-gather.13
  432.2 74.5 all-gather.11
  509.3 69.1 all-gather.17
  580.3 49.5 all-gather.15
